TPU v7x, 32 devices: a whole 2x2x4 slice. The times are simulated.
32 devices in a mesh: dom: 2 (over y), blk: 4 (over z), sub: 2 (over x), rep: 2 (over core).
Axes of the slice: x: 2, y: 2, z: 4, core: 2. Of those that a mesh axis runs over, the one named last changes fastest.
Arguments:
- tokens: bfloat16 [4096, 2048], P(('dom', 'blk', 'sub', 'rep')), parts along dimension 0, may hold values from -6 to 6
- expert_ids: int32 [4096, 8], P(('dom', 'blk', 'sub', 'rep')), parts along dimension 0, may hold values from 0 to 127, as said below
- gate_weights: float32 [4096, 8], P(('dom', 'blk', 'sub', 'rep')), parts along dimension 0, may hold values from 0.2 to 2
- w_gate: bfloat16 [2, 768, 2048], P('sub', 'rep', 'blk'), may hold values from -0.125 to 0.125
- w_up: bfloat16 [2, 768, 2048], P('sub', 'rep', 'blk'), may hold values from -0.125 to 0.125
- w_down: bfloat16 [2, 768, 2048], P('sub', 'rep', 'blk'), may hold values from -0.21875 to 0.21875
- cotangent: bfloat16 [4096, 2048], P(('dom', 'blk', 'sub', 'rep')), parts along dimension 0, may hold values from -6 to 6
Outputs:
- mixed: bfloat16 [4096, 2048], P(('dom', 'blk', 'sub', 'rep')), parts along dimension 0
- token_grad: bfloat16 [4096, 2048], P(('dom', 'blk', 'sub', 'rep')), parts along dimension 0
- gate_grad: float32 [4096, 8], P(('dom', 'blk', 'sub', 'rep')), parts along dimension 0
- grad_gate: float32 [4, 768, 2048], P(('dom', 'sub'), 'rep', 'blk'), parts along dimension 0
- grad_up: float32 [4, 768, 2048], P(('dom', 'sub'), 'rep', 'blk'), parts along dimension 0
- grad_down: float32 [4, 768, 2048], P(('dom', 'sub'), 'rep', 'blk'), parts along dimension 0
There are 2 independent parts, one for each index of `dom`. A program takes and returns all parts, laid end to end along the dimension named above; an argument that names none is the same for every part. Nothing has to cross between parts.
Inputs may be any that keep to these rules, and one draw needn't show every extreme that they name: `expert_ids`: each row names 8 different experts. Among the 128 rows of one device, each expert below 2 is named by 1 to 12 rows, and in every draw some expert below 2 is named by 12 rows on every device of one blk index.
All inputs are finite; a program needn't handle non-finite values.
Results may differ from a plain program's by a relative error of at most 0.02.
Values may be sent and summed in bfloat16 or wider, within the bound.
No kernel may reach another device: no remote copies, remote signals or barrier semaphores. Data moves between devices by JAX's collectives and lax.ppermute only.
A program may use at most 64 MiB of HBM per device.

v0:
```python
import jax
import jax.numpy as jnp
from jax import lax
from jax.sharding import PartitionSpec as P

NUM_EXPERTS = 128
TOPK = 8
CAP = 12


def silu_pair(pre_act):
    sigmoid_v = jax.nn.sigmoid(pre_act)
    return (pre_act * sigmoid_v, sigmoid_v * (1.0 + pre_act * (1.0 - sigmoid_v)))


def on_device(tokens, expert_ids, gate_weights, w_gate, w_up, w_down, cotangent):
    tok_count = tokens.shape[0]
    local_experts = w_gate.shape[0]
    n_window = local_experts * lax.axis_size("sub")
    capacity = CAP
    total_tokens = tok_count * lax.axis_size("blk") * lax.axis_size("sub") * lax.axis_size("rep")
    grad_scale = (total_tokens * TOPK / NUM_EXPERTS) ** (-0.5)
    zero_low = jnp.zeros((), jnp.bfloat16)
    expert_iota = lax.iota(jnp.int32, n_window)
    named_hits = expert_ids[:, :, None] == expert_iota[None, None, :]
    picked = jnp.sum(named_hits.astype(jnp.int32), axis=1)
    weight_of = jnp.sum(jnp.where(named_hits, gate_weights[:, :, None], 0.0), axis=1)
    before = jnp.cumsum(picked, axis=0) - picked
    slot_iota = lax.iota(jnp.int32, capacity)
    placed = (before[None, :, :] == slot_iota[:, None, None]) & (picked[None, :, :] > 0)
    row_iota = lax.iota(jnp.int32, tok_count)
    slot_row = jnp.sum(jnp.where(placed, row_iota[None, :, None], 0), axis=1)
    slot_live = jnp.any(placed, axis=1)
    slot_gate = jnp.sum(jnp.where(placed, weight_of[None, :, :], 0.0), axis=1)
    slot_tokens = jnp.where(slot_live[:, :, None], tokens[slot_row], zero_low)
    slot_cotan = jnp.where(slot_live[:, :, None], cotangent[slot_row], zero_low)
    slot_dout = (slot_cotan.astype(jnp.float32) * slot_gate[:, :, None]).astype(jnp.bfloat16)
    rows_mine, dout_mine = (
        lax.all_to_all(slot_tokens, "sub", split_axis=1, concat_axis=0, tiled=True),
        lax.all_to_all(slot_dout, "sub", split_axis=1, concat_axis=0, tiled=True),
    )
    rows_all, dout_all = (
        lax.all_gather(rows_mine, "rep", axis=0, tiled=True),
        lax.all_gather(dout_mine, "rep", axis=0, tiled=True),
    )
    full_gate, full_up, full_down = (
        lax.all_gather(w_gate, "blk", axis=2, tiled=True),
        lax.all_gather(w_up, "blk", axis=2, tiled=True),
        lax.all_gather(w_down, "blk", axis=2, tiled=True),
    )
    pre_gate = jnp.einsum("red,efd->ref", rows_all, full_gate, preferred_element_type=jnp.float32)
    pre_up = jnp.einsum("red,efd->ref", rows_all, full_up, preferred_element_type=jnp.float32)
    activated, silu_slope = silu_pair(pre_gate)
    hidden = (activated * pre_up).astype(jnp.bfloat16)
    out_sum = lax.psum_scatter(
        jnp.einsum("ref,efd->red", hidden, full_down, preferred_element_type=jnp.float32).astype(
            jnp.bfloat16
        ),
        "rep",
        scatter_dimension=0,
        tiled=True,
    )
    slot_out = lax.all_to_all(out_sum, "sub", split_axis=0, concat_axis=1, tiled=True)
    down_term = (
        jnp.einsum("ref,red->efd", hidden, dout_all, preferred_element_type=jnp.float32)
        * grad_scale
    ).astype(jnp.bfloat16)
    down_back = lax.all_to_all(down_term[None], "blk", split_axis=3, concat_axis=0, tiled=True)
    down_owned = jnp.sum(down_back.astype(jnp.float32), axis=0)
    placed_low = placed.astype(jnp.bfloat16)
    mixed_acc = jnp.zeros((tok_count, tokens.shape[1]), jnp.float32)
    for expert in range(n_window):
        picked_rows = jnp.einsum(
            "ct,cd->td",
            placed_low[:, :, expert],
            slot_out[:, expert],
            preferred_element_type=jnp.float32,
        )
        mixed_acc = mixed_acc + weight_of[:, expert : expert + 1] * picked_rows
    mixed = mixed_acc.astype(jnp.bfloat16)
    slot_dot = jnp.sum(slot_cotan.astype(jnp.float32) * slot_out.astype(jnp.float32), axis=2)
    token_dot = jnp.sum(jnp.where(placed, slot_dot[:, None, :], 0.0), axis=0)
    gate_grad = jnp.sum(jnp.where(named_hits, token_dot[:, None, :], 0.0), axis=2)
    dhidden = jnp.einsum("red,efd->ref", dout_all, full_down, preferred_element_type=jnp.float32)
    dpre_gate = (dhidden * pre_up * silu_slope).astype(jnp.bfloat16)
    dpre_up = (dhidden * activated).astype(jnp.bfloat16)
    first = jnp.einsum("ref,efd->red", dpre_gate, full_gate, preferred_element_type=jnp.float32)
    in_sum = lax.psum_scatter(
        (
            first + jnp.einsum("ref,efd->red", dpre_up, full_up, preferred_element_type=jnp.float32)
        ).astype(jnp.bfloat16),
        "rep",
        scatter_dimension=0,
        tiled=True,
    )
    slot_in = lax.all_to_all(in_sum, "sub", split_axis=0, concat_axis=1, tiled=True)
    token_grad = jnp.einsum(
        "cte,ced->td", placed_low, slot_in, preferred_element_type=jnp.float32
    ).astype(jnp.bfloat16)
    both_pre = jnp.stack([dpre_gate, dpre_up])
    proj_term = (
        jnp.einsum("gref,red->gefd", both_pre, rows_all, preferred_element_type=jnp.float32)
        * grad_scale
    ).astype(jnp.bfloat16)
    proj_back = lax.all_to_all(proj_term[None], "blk", split_axis=4, concat_axis=0, tiled=True)
    proj_owned = jnp.sum(proj_back.astype(jnp.float32), axis=0)
    grad_gate = proj_owned[0]
    grad_up = proj_owned[1]
    return (mixed, token_grad, gate_grad, grad_gate, grad_up, down_owned)


def solution(mesh):
    in_specs = (
        P(("dom", "blk", "sub", "rep"), None),
        P(("dom", "blk", "sub", "rep"), None),
        P(("dom", "blk", "sub", "rep"), None),
        P("sub", "rep", "blk"),
        P("sub", "rep", "blk"),
        P("sub", "rep", "blk"),
        P(("dom", "blk", "sub", "rep"), None),
    )
    out_specs = (
        P(("dom", "blk", "sub", "rep"), None),
        P(("dom", "blk", "sub", "rep"), None),
        P(("dom", "blk", "sub", "rep"), None),
        P(("dom", "sub"), "rep", "blk"),
        P(("dom", "sub"), "rep", "blk"),
        P(("dom", "sub"), "rep", "blk"),
    )
    return jax.shard_map(
        on_device, mesh=mesh, in_specs=in_specs, out_specs=out_specs, check_vma=False
    )
```

profile of v0, /device:TPU:0, one launch (start us, length us, event | category | flops | bytes accessed | tf_op | source)
XLA Modules:
  0.0 349.1 jit_solution(12591786999858448248)
XLA Ops:
  7.2 0.7 all-gather.6.cloned.1.call-update
  8.0 0.7 all-gather.4.cloned.1.call-update
  8.7 0.7 all-gather.8.cloned.1.call-update
  9.4 0.7 convert_reduce_fusion.1
  10.1 0.1 copy.58
  10.3 0.2 reduce_window_sum.11
  10.5 0.1 select_reduce_fusion.2
  10.7 0.1 copy.61
  10.9 0.6 gather_fusion
  11.6 0.1 fusion.41
  11.8 8.5 %all_to_all.90 = bf16[12,2,2048]{2,0,1:T(8,128)(2,1)S(1)} all-to-all(bf16[12,2,2048]{2,0,1:T(8,128)(2,1)S(1)} %copy_select_fusion.1), channel_id=1, replica_groups=mesh['dom'=2,'blk'=4,'sub'=2,'rep'=2] {'sub'}, dimensions={1} | all-to-all | bytes 196608 | tf_op jit(solution)/shard_map/all_to_all | solution.py:39
  20.3 1.9 all_gather.15
  22.3 27.1 %all-gather.6.cloned.1.call-done = bf16[1,384,2048]{2,1,0:T(8,128)(2,1)} async-done(((bf16[1,384,512]{2,1,0:T(8,128)(2,1)}), bf16[1,384,2048]{2,1,0:T(8,128)(2,1)}) %all-gather.6.cloned.1.call-update) | async-done | bytes 1572880 | tf_op jit(solution)/shard_map/all_gather | solution.py:48
  49.3 2.0 fusion.21
  51.3 35.5 %all-gather.4.cloned.1.call-done = bf16[1,384,2048]{2,1,0:T(8,128)(2,1)} async-done(((bf16[1,384,512]{2,1,0:T(8,128)(2,1)}), bf16[1,384,2048]{2,1,0:T(8,128)(2,1)}) %all-gather.4.cloned.1.call-update) | async-done | bytes 1572880 | tf_op jit(solution)/shard_map/all_gather | solution.py:47
  86.8 2.0 fusion.18
  88.9 35.5 %all-gather.8.cloned.1.call-done = bf16[1,384,2048]{2,1,0:T(8,128)(2,1)} async-done(((bf16[1,384,512]{2,1,0:T(8,128)(2,1)}), bf16[1,384,2048]{2,1,0:T(8,128)(2,1)}) %all-gather.8.cloned.1.call-update) | async-done | bytes 1572880 | tf_op jit(solution)/shard_map/all_gather | solution.py:49
  124.3 2.5 fusion.6
  126.8 6.7 %reduce-scatter.3.cloned.1.call-done = bf16[24,1,2048]{2,0,1:T(8,128)(2,1)} async-done(((bf16[48,1,2048]{2,0,1:T(8,128)(2,1)}), bf16[24,1,2048]{2,0,1:T(8,128)(2,1)}) %reduce-scatter.3.cloned.1.call-update) | async-done | bytes 98320 | tf_op jit(solution)/shard_map/reduce_scatter | solution.py:55
  133.5 0.5 broadcast.59
  134.0 1.6 reduce.10
  135.6 0.8 reshape.167
  136.4 3.3 all-to-all-start.1
  139.8 0.6 gather_fusion.1
  140.5 3.5 %all-to-all-done.1 = bf16[2,2,12288]{2,1,0:T(2,128)(2,1)S(1)} async-done(((bf16[2,2,12288]{2,1,0:T(2,128)(2,1)}), bf16[2,2,12288]{2,1,0:T(2,128)(2,1)S(1)}, u32[]{:S(2)}, u32[]{:S(2)}) %all-to-all-start.1) | async-done | bytes 98336 | tf_op jit(solution)/shard_map/all_to_all | solution.py:63
  144.0 0.1 reshape.168
  144.1 0.5 reduce.8
  144.7 0.2 fusion.28
  144.9 0.1 select_reduce_fusion
  145.0 0.6 select_reduce_fusion.3
  145.6 0.1 select_reduce_fusion.1
  145.7 0.1 fusion.27
  145.8 6.8 %all_to_all.91 = bf16[12,2,2048]{2,0,1:T(8,128)(2,1)S(1)} all-to-all(bf16[12,2,2048]{2,0,1:T(8,128)(2,1)S(1)} %fusion.27), channel_id=1, replica_groups=mesh['dom'=2,'blk'=4,'sub'=2,'rep'=2] {'sub'}, dimensions={1} | all-to-all | bytes 196608 | tf_op jit(solution)/shard_map/all_to_all | solution.py:40
  152.6 1.9 all_gather.19
  154.6 2.1 multiply_convert_fusion.2
  156.7 0.4 fusion.14
  157.1 1.1 fusion.7
  158.2 8.0 %reduce-scatter.5.cloned.1.call-done = bf16[24,1,2048]{2,0,1:T(8,128)(2,1)} async-done(((bf16[48,1,2048]{2,0,1:T(8,128)(2,1)}), bf16[24,1,2048]{2,0,1:T(8,128)(2,1)}) %reduce-scatter.5.cloned.1.call-update) | async-done | bytes 98320 | tf_op jit(solution)/shard_map/reduce_scatter | solution.py:88
  166.2 1.6 reduce.11
  167.8 0.8 reshape.171
  168.6 3.3 all-to-all-start.3
  171.9 0.6 fusion.1
  172.5 5.6 %copy.68 = bf16[1,1,384,2048]{2,1,0,3:T(2,128)(2,1)} copy(bf16[1,1,384,2048]{3,2,1,0:T(8,128)(2,1)S(1)} %fusion.1) | data formatting | bytes 3145728 | tf_op jit(solution)/shard_map/broadcast_in_dim | solution.py:68
  178.1 34.3 %reduce.12 = bf16[2048,384]{1,0:T(8,128)(2,1)S(1)} reduce(bf16[2048,1,1,384]{3,2,1,0:T(2,128)(2,1)} %bitcast.140, bf16[]{:T(256)} %broadcast.59), dimensions={1,2}, to_apply=%bitcast.132.reduce_sub_computation | reduce | bytes 3145730
  212.4 1.9 reshape.169
  214.3 4.8 %all-to-all-start.5 = ((bf16[4,2,98304]{2,1,0:T(2,128)(2,1)}), bf16[4,2,98304]{2,1,0:T(2,128)(2,1)S(1)}, u32[]{:S(2)}, u32[]{:S(2)}) async-start(bf16[4,2,98304]{2,1,0:T(2,128)(2,1)} %reshape.169), calls=%async_computation.7 | async-start | bytes 3145728 | tf_op jit(solution)/shard_map/all_to_all | solution.py:68
  219.1 1.0 fusion
  220.1 28.4 %copy.66 = bf16[1,2,1,384,2048]{3,1,2,0,4:T(2,128)(2,1)} copy(bf16[1,2,1,384,2048]{3,4,1,2,0:T(8,128)(2,1)S(1)} %fusion) | data formatting | bytes 6291456 | tf_op jit(solution)/shard_map/broadcast_in_dim | solution.py:105
  248.6 8.0 %all-to-all-done.5 = bf16[4,2,98304]{2,1,0:T(2,128)(2,1)S(1)} async-done(((bf16[4,2,98304]{2,1,0:T(2,128)(2,1)}), bf16[4,2,98304]{2,1,0:T(2,128)(2,1)S(1)}, u32[]{:S(2)}, u32[]{:S(2)}) %all-to-all-start.5) | async-done | bytes 1572896 | tf_op jit(solution)/shard_map/all_to_all | solution.py:68
  256.6 4.9 %all-to-all-start.4 = ((bf16[1,2,1,384,2048]{3,1,2,0,4:T(2,128)(2,1)}), bf16[1,2,1,384,2048]{3,1,2,0,4:T(2,128)(2,1)}, u32[]{:S(2)}, u32[]{:S(2)}) async-start(bf16[1,2,1,384,2048]{3,1,2,0,4:T(2,128)(2,1)} %copy.66), calls=%async_computation.6 | async-start | bytes 6291456 | tf_op jit(solution)/shard_map/all_to_all | solution.py:105
  261.5 0.3 convolution_multiply_fusion.1
  261.8 1.1 fusion.3
  263.0 0.1 reshape.172
  263.1 0.5 reduce.9
  263.7 1.1 fusion.4
  264.8 2.9 reshape.170
  267.7 3.7 %copy.74 = f32[1,1,384,2048]{2,3,0,1:T(8,128)} copy(bf16[1,1,384,2048]{2,1,0,3:T(2,128)(2,1)} %bitcast.142) | data formatting | bytes 4718592
  271.4 2.1 reduce_sum.94
  273.5 1.1 copy.71
  274.7 56.9 %all-to-all-done.4 = bf16[1,2,1,384,2048]{3,1,2,0,4:T(2,128)(2,1)} async-done(((bf16[1,2,1,384,2048]{3,1,2,0,4:T(2,128)(2,1)}), bf16[1,2,1,384,2048]{3,1,2,0,4:T(2,128)(2,1)}, u32[]{:S(2)}, u32[]{:S(2)}) %all-to-all-start.4) | async-done | bytes 3145760 | tf_op jit(solution)/shard_map/all_to_all | solution.py:105
  331.6 5.7 %convert_reduce_fusion = f32[2,384,512]{1,0,2:T(2,128)S(1)} fusion(bf16[2,384,4,512]{1,0,3,2:T(2,128)(2,1)} %bitcast.65), kind=kLoop, calls=%fused_computation.2 | loop fusion | flops 2752512 | bytes 4718592 | tf_op jit(solution)/shard_map/reduce_sum | solution.py:106
  337.3 1.2 fusion.45
  338.5 2.1 copy.70
  340.6 2.0 copy.69
  (35 shorter events, 0.8 us)
Async XLA Ops:
  7.2 3.7 %copy-start = (bf16[128,2048]{1,0:T(8,128)(2,1)S(1)}, bf16[128,2048]{1,0:T(8,128)(2,1)}, u32[]{:S(2)}) copy-start(bf16[128,2048]{1,0:T(8,128)(2,1)} %param.7) | copy-start | bytes 1572868
  7.2 42.2 %all-gather.6.cloned.1.call-start = ((), (), s32[]{:S(2)}) async-start(), calls=%async_computation.9 | async-start | bytes 1966080 | tf_op jit(solution)/shard_map/all_gather | solution.py:48
  7.9 78.9 %all-gather.4.cloned.1.call-start = ((), (), s32[]{:S(2)}) async-start(), calls=%async_computation.8 | async-start | bytes 1966080 | tf_op jit(solution)/shard_map/all_gather | solution.py:47
  8.7 115.7 %all-gather.8.cloned.1.call-start = ((), (), s32[]{:S(2)}) async-start(), calls=%async_computation.10 | async-start | bytes 1966080 | tf_op jit(solution)/shard_map/all_gather | solution.py:49
  9.4 124.1 %reduce-scatter.3.cloned.1.call-start = ((), (), s32[]{:S(2)}) async-start(), calls=%async_computation.11 | async-start | bytes 294912 | tf_op jit(solution)/shard_map/reduce_scatter | solution.py:55
  88.8 50.9 %copy-start.3 = (bf16[128,2048]{1,0:T(8,128)(2,1)S(1)}, bf16[128,2048]{1,0:T(8,128)(2,1)}, u32[]{:S(2)}) copy-start(bf16[128,2048]{1,0:T(8,128)(2,1)} %param.13) | copy-start | bytes 1572868
  126.8 18.2 %copy-start.4 = (s32[128,8]{0,1:T(8,128)S(1)}, s32[128,8]{0,1:T(8,128)}, u32[]{:S(2)}) copy-start(s32[128,8]{0,1:T(8,128)} %param.8) | copy-start | bytes 12292
  126.8 18.2 %copy-start.5 = (f32[128,8]{0,1:T(8,128)S(1)}, f32[128,8]{0,1:T(8,128)}, u32[]{:S(2)}) copy-start(f32[128,8]{0,1:T(8,128)} %param.9) | copy-start | bytes 12292
  136.4 7.6 %all-to-all-start.1 = ((bf16[2,2,12288]{2,1,0:T(2,128)(2,1)}), bf16[2,2,12288]{2,1,0:T(2,128)(2,1)S(1)}, u32[]{:S(2)}, u32[]{:S(2)}) async-start(bf16[2,2,12288]{2,1,0:T(2,128)(2,1)} %reshape.167), calls=%async_computation.2 | async-start | bytes 196608 | tf_op jit(solution)/shard_map/all_to_all | solution.py:63
  139.7 26.5 %reduce-scatter.5.cloned.1.call-start = ((), (), s32[]{:S(2)}) async-start(), calls=%async_computation.12 | async-start | bytes 294912 | tf_op jit(solution)/shard_map/reduce_scatter | solution.py:88
  144.8 11.9 %copy-start.2 = (bf16[1,384,2048]{2,1,0:T(8,128)(2,1)S(1)}, bf16[1,384,2048]{2,1,0:T(8,128)(2,1)}, u32[]{:S(2)}) copy-start(bf16[1,384,2048]{2,1,0:T(8,128)(2,1)} %all-gather.4.cloned.1.call-done) | copy-start | bytes 4718596
  154.6 2.5 copy-start.1
  168.6 45.7 %all-to-all-start.3 = ((bf16[2,2,12288]{2,1,0:T(2,128)(2,1)}), bf16[2,2,12288]{2,1,0:T(2,128)(2,1)S(1)}, u32[]{:S(2)}, u32[]{:S(2)}) async-start(bf16[2,2,12288]{2,1,0:T(2,128)(2,1)} %reshape.171), calls=%async_computation.5 | async-start | bytes 196608 | tf_op jit(solution)/shard_map/all_to_all | solution.py:96
  214.3 42.3 %all-to-all-start.5 = ((bf16[4,2,98304]{2,1,0:T(2,128)(2,1)}), bf16[4,2,98304]{2,1,0:T(2,128)(2,1)S(1)}, u32[]{:S(2)}, u32[]{:S(2)}) async-start(bf16[4,2,98304]{2,1,0:T(2,128)(2,1)} %reshape.169), calls=%async_computation.7 | async-start | bytes 3145728 | tf_op jit(solution)/shard_map/all_to_all | solution.py:68
  256.6 75.0 %all-to-all-start.4 = ((bf16[1,2,1,384,2048]{3,1,2,0,4:T(2,128)(2,1)}), bf16[1,2,1,384,2048]{3,1,2,0,4:T(2,128)(2,1)}, u32[]{:S(2)}, u32[]{:S(2)}) async-start(bf16[1,2,1,384,2048]{3,1,2,0,4:T(2,128)(2,1)} %copy.66), calls=%async_computation.6 | async-start | bytes 6291456 | tf_op jit(solution)/shard_map/all_to_all | solution.py:105
Sparse Core Ops, SparseCore 0:
  9.6 39.7 all-gather.5
  50.9 35.8 all-gather.3
  88.4 35.8 all-gather.7
  127.0 6.4 reduce-scatter.2
  158.3 7.8 reduce-scatter.4
where the time goes:
time: 350 us; the launch traced here: 349 us
  waiting for transfers between devices  183 us (52%)
  local copies, waits for them, and re-layouts  53.1 us (15%)
  other arithmetic  48.7 us (14%)
  blocking collectives  19.3 us (6%)
  starting transfers between devices  16.5 us (5%)
  matrix products  14.2 us (4%)
  between operations  14.1 us (4%)
    all_to_all x1, waiting for transfers between devices, on_device(): lax.all_to_all(proj_term[None], 'blk', split_axis=4, concat_axis=0, tiled...  56.9 us
    all_gather x1, waiting for transfers between devices, on_device(): lax.all_gather(w_gate, 'blk', axis=2, tiled=True)  35.5 us
    all_gather x1, waiting for transfers between devices, on_device(): lax.all_gather(w_down, 'blk', axis=2, tiled=True)  35.5 us
    unnamed x1, other arithmetic  34.3 us
    broadcast_in_dim x1, local copies, waits for them, and re-layouts, on_device(): proj_term[None]  28.4 us
    all_gather x1, waiting for transfers between devices, on_device(): lax.all_gather(w_up, 'blk', axis=2, tiled=True)  27.1 us
    unnamed x22, local copies, waits for them, and re-layouts  15.4 us
    all_to_all x1, blocking collectives, on_device(): lax.all_to_all(slot_tokens, 'sub', split_axis=1, concat_axis=0, tiled=True)  8.51 us
  transfers between devices with their start and end apart: 9, of which 8 were waited for; matrix products, arithmetic and copies ran while one was open for 26% of the time, Pallas kernels for 0%

commit v1 on v0

--- a/solution.py
+++ b/solution.py
@@ -6,6 +6,28 @@
 NUM_EXPERTS = 128
 TOPK = 8
 CAP = 12
+
+
+def laid_out(parts, dim):
+    parts = jnp.moveaxis(parts, 0, dim)
+    shape = parts.shape
+    return parts.reshape(*shape[:dim], shape[dim] * shape[dim + 1], *shape[dim + 2 :])
+
+
+def collect(x, axis, dim):
+    length = lax.axis_size(axis)
+    pairs = [(i, (i + 1) % length) for i in range(length)]
+    back = [(b, a) for a, b in pairs]
+    lower, upper = ([], [])
+    for hop in range(length - 1):
+        if hop % 2 == 0:
+            lower.append(lax.ppermute(lower[-1] if lower else x, axis, pairs))
+        else:
+            upper.append(lax.ppermute(upper[-1] if upper else x, axis, back))
+    pieces = jnp.stack([*lower[::-1], x, *upper])
+    shift = lax.axis_index(axis) - len(lower)
+    pieces = pieces[(jnp.arange(length) - shift) % length]
+    return laid_out(pieces, dim)
 
 
 def silu_pair(pre_act):
@@ -45,7 +67,7 @@
     )
     full_gate, full_up, full_down = (
         lax.all_gather(w_gate, "blk", axis=2, tiled=True),
-        lax.all_gather(w_up, "blk", axis=2, tiled=True),
+        collect(w_up, "blk", 2),
         lax.all_gather(w_down, "blk", axis=2, tiled=True),
     )
     pre_gate = jnp.einsum("red,efd->ref", rows_all, full_gate, preferred_element_type=jnp.float32)

time: 350 us -> 329 us (0.940)
  waiting for transfers between devices: 183 us -> 157 us
  starting transfers between devices: 16.5 us -> 25.3 us
  blocking collectives: 19.3 us -> 10.9 us
  local copies, waits for them, and re-layouts: 53.1 us -> 57.5 us
    all_gather x1, waiting for transfers between devices: 35.5 us -> 3.94 us  [on_device(): lax.all_gather(w_gate, 'blk', axis=2, tiled=True)]
    ppermute x0 -> x3, waiting for transfers between devices: none -> 28.7 us  [the longest x1 19.5 us: collect(): upper.append(lax.ppermute(upper[-1] if upper else x, axis, back))]
    all_gather x1 -> x0, waiting for transfers between devices: 27.1 us -> none  [on_device(): lax.all_gather(w_up, 'blk', axis=2, tiled=True)]
    all_to_all x1 -> x0, blocking collectives: 8.51 us -> none  [on_device(): lax.all_to_all(slot_tokens, 'sub', split_axis=1, concat_axis=0, tiled=True)]
    ppermute x0 -> x3, starting transfers between devices: none -> 5.47 us  [the longest x2 3.38 us: collect(): lower.append(lax.ppermute(lower[-1] if lower else x, axis, pairs))]
    all_to_all x0 -> x1, waiting for transfers between devices: none -> 4.37 us  [on_device(): lax.all_to_all(slot_tokens, 'sub', split_axis=1, concat_axis=0, tiled=True)]
    unnamed x22 -> x24, local copies, waits for them, and re-layouts: 15.4 us -> 16.2 us
  transfers between devices with their start and end apart: 9 -> 12, of which waited for: 8 -> 11; matrix products, arithmetic and copies ran while one was open for 26% -> 29% of each run, Pallas kernels for 0% -> 0%
where the time goes in v1:
time: 329 us; the launch traced here: 328 us
  waiting for transfers between devices  157 us (48%)
  local copies, waits for them, and re-layouts  57.5 us (17%)
  other arithmetic  50.5 us (15%)
  starting transfers between devices  25.3 us (8%)
  between operations  14.1 us (4%)
  matrix products  12.7 us (4%)
  blocking collectives  10.9 us (3%)
    all_to_all x1, waiting for transfers between devices, on_device(): lax.all_to_all(proj_term[None], 'blk', split_axis=4, concat_axis=0, tiled...  57.2 us
    all_gather x1, waiting for transfers between devices, on_device(): lax.all_gather(w_down, 'blk', axis=2, tiled=True)  35.9 us
    unnamed x1, other arithmetic  34.3 us
    broadcast_in_dim x1, local copies, waits for them, and re-layouts, on_device(): proj_term[None]  28.4 us
    ppermute x1, waiting for transfers between devices, collect(): upper.append(lax.ppermute(upper[-1] if upper else x, axis, back))  19.5 us
    unnamed x24, local copies, waits for them, and re-layouts  16.2 us
    ppermute x2, waiting for transfers between devices, collect(): lower.append(lax.ppermute(lower[-1] if lower else x, axis, pairs))  9.22 us
    all_to_all x1, waiting for transfers between devices, on_device(): lax.all_to_all(down_term[None], 'blk', split_axis=3, concat_axis=0, tiled...  8.04 us
  transfers between devices with their start and end apart: 12, of which 11 were waited for; matrix products, arithmetic and copies ran while one was open for 29% of the time, Pallas kernels for 0%

profile of v1, /device:TPU:0, one launch (start us, length us, event | category | flops | bytes accessed | tf_op | source)
XLA Modules:
  0.0 328.3 jit_solution(10544516583501412706)
XLA Ops:
  7.2 0.7 all-gather.3.cloned.1.call-update
  8.0 3.1 collective-permute-start
  11.1 2.1 collective-permute-start.2
  13.2 0.7 convert_reduce_fusion.1
  14.0 0.2 reduce_window_sum.11
  14.6 0.6 gather_fusion
  15.4 7.9 %collective-permute-done = bf16[1,384,512]{2,1,0:T(8,128)(2,1)S(1)} collective-permute-done((bf16[1,384,512]{2,1,0:T(8,128)(2,1)}, bf16[1,384,512]{2,1,0:T(8,128)(2,1)S(1)}, u32[]{:S(2)}, u32[]{:S(2)}) %collective-permute-start) | collective-permute-done | bytes 393248 | tf_op jit(solution)/shard_map/ppermute | solution.py:24
  23.3 0.3 collective-permute-start.1
  23.6 0.7 copy_select_fusion.1
  24.3 3.4 %all-to-all-start = ((bf16[12,2,2048]{2,0,1:T(8,128)(2,1)}), bf16[12,2,2048]{2,0,1:T(8,128)(2,1)S(1)}, u32[]{:S(2)}, u32[]{:S(2)}) async-start(bf16[12,2,2048]{2,0,1:T(8,128)(2,1)} %copy_select_fusion.1), calls=%async_computation | async-start | bytes 262144 | tf_op jit(solution)/shard_map/all_to_all | solution.py:61
  27.8 4.4 %all-to-all-done = bf16[12,2,2048]{2,0,1:T(8,128)(2,1)S(1)} async-done(((bf16[12,2,2048]{2,0,1:T(8,128)(2,1)}), bf16[12,2,2048]{2,0,1:T(8,128)(2,1)S(1)}, u32[]{:S(2)}, u32[]{:S(2)}) %all-to-all-start) | async-done | bytes 98336 | tf_op jit(solution)/shard_map/all_to_all | solution.py:61
  32.2 1.9 all_gather.12
  34.2 19.5 %collective-permute-done.2 = bf16[1,384,512]{2,1,0:T(8,128)(2,1)S(1)} collective-permute-done((bf16[1,384,512]{2,1,0:T(8,128)(2,1)}, bf16[1,384,512]{2,1,0:T(8,128)(2,1)S(1)}, u32[]{:S(2)}, u32[]{:S(2)}) %collective-permute-start.2) | collective-permute-done | bytes 393248 | tf_op jit(solution)/shard_map/ppermute | solution.py:26
  53.6 1.3 collective-permute-done.1
  55.0 0.7 copy-done.4
  55.7 1.2 maximum_bitcast_fusion
  56.9 1.8 gather_fusion.1
  58.7 1.9 copy.77
  60.6 0.4 convolution_bitcast_fusion.2
  61.0 3.9 %all-gather.3.cloned.1.call-done = bf16[1,384,2048]{2,1,0:T(8,128)(2,1)} async-done(((bf16[1,384,512]{2,1,0:T(8,128)(2,1)}), bf16[1,384,2048]{2,1,0:T(8,128)(2,1)}) %all-gather.3.cloned.1.call-update) | async-done | bytes 1572880 | tf_op jit(solution)/shard_map/all_gather | solution.py:69
  64.9 2.0 fusion.14
  67.0 35.9 %all-gather.5.cloned.1.call-done = bf16[1,384,2048]{2,1,0:T(8,128)(2,1)} async-done(((bf16[1,384,512]{2,1,0:T(8,128)(2,1)}), bf16[1,384,2048]{2,1,0:T(8,128)(2,1)}) %all-gather.5.cloned.1.call-update) | async-done | bytes 1572880 | tf_op jit(solution)/shard_map/all_gather | solution.py:71
  102.9 2.5 fusion.6
  105.4 6.8 %reduce-scatter.3.cloned.1.call-done = bf16[24,1,2048]{2,0,1:T(8,128)(2,1)} async-done(((bf16[48,1,2048]{2,0,1:T(8,128)(2,1)}), bf16[24,1,2048]{2,0,1:T(8,128)(2,1)}) %reduce-scatter.3.cloned.1.call-update) | async-done | bytes 98320 | tf_op jit(solution)/shard_map/reduce_scatter | solution.py:77
  112.3 0.5 broadcast.128
  112.8 1.6 reduce.10
  114.3 0.8 reshape.231
  115.1 3.3 %all-to-all-start.1 = ((bf16[2,2,12288]{2,1,0:T(2,128)(2,1)}), bf16[2,2,12288]{2,1,0:T(2,128)(2,1)S(1)}, u32[]{:S(2)}, u32[]{:S(2)}) async-start(bf16[2,2,12288]{2,1,0:T(2,128)(2,1)} %reshape.231), calls=%async_computation.2 | async-start | bytes 196608 | tf_op jit(solution)/shard_map/all_to_all | solution.py:85
  118.5 0.6 gather_fusion.2
  119.2 3.5 %all-to-all-done.1 = bf16[2,2,12288]{2,1,0:T(2,128)(2,1)S(1)} async-done(((bf16[2,2,12288]{2,1,0:T(2,128)(2,1)}), bf16[2,2,12288]{2,1,0:T(2,128)(2,1)S(1)}, u32[]{:S(2)}, u32[]{:S(2)}) %all-to-all-start.1) | async-done | bytes 98336 | tf_op jit(solution)/shard_map/all_to_all | solution.py:85
  122.8 0.5 reduce.8
  123.4 0.2 fusion.21
  123.7 0.6 select_reduce_fusion.3
  124.5 6.8 %all_to_all.90 = bf16[12,2,2048]{2,0,1:T(8,128)(2,1)S(1)} all-to-all(bf16[12,2,2048]{2,0,1:T(8,128)(2,1)S(1)} %fusion.20), channel_id=1, replica_groups=mesh['dom'=2,'blk'=4,'sub'=2,'rep'=2] {'sub'}, dimensions={1} | all-to-all | bytes 196608 | tf_op jit(solution)/shard_map/all_to_all | solution.py:62
  131.4 2.1 all_gather.15
  133.5 2.0 multiply_convert_fusion.2
  135.5 0.4 convolution_bitcast_fusion.1
  135.9 1.3 fusion.7
  137.2 8.0 %reduce-scatter.5.cloned.1.call-done = bf16[24,1,2048]{2,0,1:T(8,128)(2,1)} async-done(((bf16[48,1,2048]{2,0,1:T(8,128)(2,1)}), bf16[24,1,2048]{2,0,1:T(8,128)(2,1)}) %reduce-scatter.5.cloned.1.call-update) | async-done | bytes 98320 | tf_op jit(solution)/shard_map/reduce_scatter | solution.py:110
  145.2 1.6 reduce.11
  146.8 0.8 reshape.235
  147.5 3.3 %all-to-all-start.3 = ((bf16[2,2,12288]{2,1,0:T(2,128)(2,1)}), bf16[2,2,12288]{2,1,0:T(2,128)(2,1)S(1)}, u32[]{:S(2)}, u32[]{:S(2)}) async-start(bf16[2,2,12288]{2,1,0:T(2,128)(2,1)} %reshape.235), calls=%async_computation.5 | async-start | bytes 196608 | tf_op jit(solution)/shard_map/all_to_all | solution.py:118
  150.9 0.6 fusion.1
  151.4 5.6 %copy.83 = bf16[1,1,384,2048]{2,1,0,3:T(2,128)(2,1)} copy(bf16[1,1,384,2048]{3,2,1,0:T(8,128)(2,1)S(1)} %fusion.1) | data formatting | bytes 3145728 | tf_op jit(solution)/shard_map/broadcast_in_dim | solution.py:90
  157.1 34.3 %reduce.12 = bf16[2048,384]{1,0:T(8,128)(2,1)S(1)} reduce(bf16[2048,1,1,384]{3,2,1,0:T(2,128)(2,1)} %bitcast.149, bf16[]{:T(256)} %broadcast.128), dimensions={1,2}, to_apply=%bitcast.137.reduce_sub_computation | reduce | bytes 3145730
  191.4 1.9 reshape.233
  193.3 5.0 %all-to-all-start.5 = ((bf16[4,2,98304]{2,1,0:T(2,128)(2,1)}), bf16[4,2,98304]{2,1,0:T(2,128)(2,1)S(1)}, u32[]{:S(2)}, u32[]{:S(2)}) async-start(bf16[4,2,98304]{2,1,0:T(2,128)(2,1)} %reshape.233), calls=%async_computation.7 | async-start | bytes 3145728 | tf_op jit(solution)/shard_map/all_to_all | solution.py:90
  198.3 1.0 fusion
  199.3 28.4 %copy.81 = bf16[1,2,1,384,2048]{3,1,2,0,4:T(2,128)(2,1)} copy(bf16[1,2,1,384,2048]{3,4,1,2,0:T(8,128)(2,1)S(1)} %fusion) | data formatting | bytes 6291456 | tf_op jit(solution)/shard_map/broadcast_in_dim | solution.py:127
  227.7 8.0 %all-to-all-done.5 = bf16[4,2,98304]{2,1,0:T(2,128)(2,1)S(1)} async-done(((bf16[4,2,98304]{2,1,0:T(2,128)(2,1)}), bf16[4,2,98304]{2,1,0:T(2,128)(2,1)S(1)}, u32[]{:S(2)}, u32[]{:S(2)}) %all-to-all-start.5) | async-done | bytes 1572896 | tf_op jit(solution)/shard_map/all_to_all | solution.py:90
  235.7 4.6 %all-to-all-start.4 = ((bf16[1,2,1,384,2048]{3,1,2,0,4:T(2,128)(2,1)}), bf16[1,2,1,384,2048]{3,1,2,0,4:T(2,128)(2,1)}, u32[]{:S(2)}, u32[]{:S(2)}) async-start(bf16[1,2,1,384,2048]{3,1,2,0,4:T(2,128)(2,1)} %copy.81), calls=%async_computation.6 | async-start | bytes 6291456 | tf_op jit(solution)/shard_map/all_to_all | solution.py:127
  240.4 0.3 convolution_multiply_fusion.1
  240.7 1.1 fusion.3
  242.0 0.5 reduce.9
  242.6 1.1 fusion.4
  243.7 2.9 reshape.234
  246.6 3.7 %copy.89 = f32[1,1,384,2048]{2,3,0,1:T(8,128)} copy(bf16[1,1,384,2048]{2,1,0,3:T(2,128)(2,1)} %bitcast.151) | data formatting | bytes 4718592
  250.3 2.1 reduce_sum.94
  252.5 1.1 copy.86
  253.6 57.2 %all-to-all-done.4 = bf16[1,2,1,384,2048]{3,1,2,0,4:T(2,128)(2,1)} async-done(((bf16[1,2,1,384,2048]{3,1,2,0,4:T(2,128)(2,1)}), bf16[1,2,1,384,2048]{3,1,2,0,4:T(2,128)(2,1)}, u32[]{:S(2)}, u32[]{:S(2)}) %all-to-all-start.4) | async-done | bytes 3145760 | tf_op jit(solution)/shard_map/all_to_all | solution.py:127
  310.8 5.7 %convert_reduce_fusion = f32[2,384,512]{1,0,2:T(2,128)S(1)} fusion(bf16[2,384,4,512]{1,0,3,2:T(2,128)(2,1)} %bitcast.73), kind=kLoop, calls=%fused_computation.3 | loop fusion | flops 2752512 | bytes 4718592 | tf_op jit(solution)/shard_map/reduce_sum | solution.py:128
  316.4 1.2 fusion.40
  317.7 2.1 copy.85
  319.7 2.0 copy.84
  (46 shorter events, 1.7 us)
Async XLA Ops:
  7.2 7.4 %copy-start = (bf16[128,2048]{1,0:T(8,128)(2,1)S(1)}, bf16[128,2048]{1,0:T(8,128)(2,1)}, u32[]{:S(2)}) copy-start(bf16[128,2048]{1,0:T(8,128)(2,1)} %param.7) | copy-start | bytes 1572868
  7.2 57.7 %all-gather.3.cloned.1.call-start = ((), (), s32[]{:S(2)}) async-start(), calls=%async_computation.8 | async-start | bytes 1966080 | tf_op jit(solution)/shard_map/all_gather | solution.py:69
  7.9 47.8 %copy-start.3 = (bf16[1,384,512]{2,1,0:T(8,128)(2,1)S(1)}, bf16[1,384,512]{2,1,0:T(8,128)(2,1)}, u32[]{:S(2)}) copy-start(bf16[1,384,512]{2,1,0:T(8,128)(2,1)} %param.11) | copy-start | bytes 1179652
  7.9 95.0 %all-gather.5.cloned.1.call-start = ((), (), s32[]{:S(2)}) async-start(), calls=%async_computation.9 | async-start | bytes 1966080 | tf_op jit(solution)/shard_map/all_gather | solution.py:71
  8.0 15.3 %collective-permute-start = (bf16[1,384,512]{2,1,0:T(8,128)(2,1)}, bf16[1,384,512]{2,1,0:T(8,128)(2,1)S(1)}, u32[]{:S(2)}, u32[]{:S(2)}) collective-permute-start(bf16[1,384,512]{2,1,0:T(8,128)(2,1)} %param.11), channel_id=1, source_target_pairs={{0,4},{4,8},{8,12},{12,0},{1,5},{5,9},{9,13},{13,1},{2,6},{6,10},{... | collective-permute-start | bytes 1179656 | tf_op jit(solution)/shard_map/ppermute | solution.py:24
  11.1 42.6 %collective-permute-start.2 = (bf16[1,384,512]{2,1,0:T(8,128)(2,1)}, bf16[1,384,512]{2,1,0:T(8,128)(2,1)S(1)}, u32[]{:S(2)}, u32[]{:S(2)}) collective-permute-start(bf16[1,384,512]{2,1,0:T(8,128)(2,1)} %param.11), channel_id=1, source_target_pairs={{4,0},{8,4},{12,8},{0,12},{5,1},{9,5},{13,9},{1,13},{6,2},{10,6},{... | collective-permute-start | bytes 1179656 | tf_op jit(solution)/shard_map/ppermute | solution.py:26
  23.3 31.7 %collective-permute-start.1 = (bf16[1,384,512]{2,1,0:T(8,128)(2,1)S(1)}, bf16[1,384,512]{2,1,0:T(8,128)(2,1)S(1)}, u32[]{:S(2)}, u32[]{:S(2)}) collective-permute-start(bf16[1,384,512]{2,1,0:T(8,128)(2,1)S(1)} %collective-permute-done), channel_id=1, source_target_pairs={{0,4},{4,8},{8,12},{12,0},{1,5},{5,9},{9,13},{13,1},{2,6},{6,10},{... | collective-permute-start | bytes 1179656 | tf_op jit(solution)/shard_map/ppermute | solution.py:24
  24.3 7.8 %all-to-all-start = ((bf16[12,2,2048]{2,0,1:T(8,128)(2,1)}), bf16[12,2,2048]{2,0,1:T(8,128)(2,1)S(1)}, u32[]{:S(2)}, u32[]{:S(2)}) async-start(bf16[12,2,2048]{2,0,1:T(8,128)(2,1)} %copy_select_fusion.1), calls=%async_computation | async-start | bytes 262144 | tf_op jit(solution)/shard_map/all_to_all | solution.py:61
  27.7 84.5 %reduce-scatter.3.cloned.1.call-start = ((), (), s32[]{:S(2)}) async-start(), calls=%async_computation.10 | async-start | bytes 294912 | tf_op jit(solution)/shard_map/reduce_scatter | solution.py:77
  55.0 0.7 copy-start.4
  66.9 51.6 %copy-start.2 = (bf16[128,2048]{1,0:T(8,128)(2,1)S(1)}, bf16[128,2048]{1,0:T(8,128)(2,1)}, u32[]{:S(2)}) copy-start(bf16[128,2048]{1,0:T(8,128)(2,1)} %param.13) | copy-start | bytes 1572868
  105.4 18.3 %copy-start.5 = (s32[128,8]{0,1:T(8,128)S(1)}, s32[128,8]{0,1:T(8,128)}, u32[]{:S(2)}) copy-start(s32[128,8]{0,1:T(8,128)} %param.8) | copy-start | bytes 12292
  105.4 18.3 %copy-start.6 = (f32[128,8]{0,1:T(8,128)S(1)}, f32[128,8]{0,1:T(8,128)}, u32[]{:S(2)}) copy-start(f32[128,8]{0,1:T(8,128)} %param.9) | copy-start | bytes 12292
  115.1 7.6 %all-to-all-start.1 = ((bf16[2,2,12288]{2,1,0:T(2,128)(2,1)}), bf16[2,2,12288]{2,1,0:T(2,128)(2,1)S(1)}, u32[]{:S(2)}, u32[]{:S(2)}) async-start(bf16[2,2,12288]{2,1,0:T(2,128)(2,1)} %reshape.231), calls=%async_computation.2 | async-start | bytes 196608 | tf_op jit(solution)/shard_map/all_to_all | solution.py:85
  118.4 26.8 %reduce-scatter.5.cloned.1.call-start = ((), (), s32[]{:S(2)}) async-start(), calls=%async_computation.11 | async-start | bytes 294912 | tf_op jit(solution)/shard_map/reduce_scatter | solution.py:110
  131.4 4.1 %copy-start.1 = (bf16[1,384,2048]{2,1,0:T(8,128)(2,1)S(1)}, bf16[1,384,2048]{2,1,0:T(8,128)(2,1)}, u32[]{:S(2)}) copy-start(bf16[1,384,2048]{2,1,0:T(8,128)(2,1)} %all-gather.3.cloned.1.call-done) | copy-start | bytes 4718596
  147.5 45.7 %all-to-all-start.3 = ((bf16[2,2,12288]{2,1,0:T(2,128)(2,1)}), bf16[2,2,12288]{2,1,0:T(2,128)(2,1)S(1)}, u32[]{:S(2)}, u32[]{:S(2)}) async-start(bf16[2,2,12288]{2,1,0:T(2,128)(2,1)} %reshape.235), calls=%async_computation.5 | async-start | bytes 196608 | tf_op jit(solution)/shard_map/all_to_all | solution.py:118
  193.3 42.5 %all-to-all-start.5 = ((bf16[4,2,98304]{2,1,0:T(2,128)(2,1)}), bf16[4,2,98304]{2,1,0:T(2,128)(2,1)S(1)}, u32[]{:S(2)}, u32[]{:S(2)}) async-start(bf16[4,2,98304]{2,1,0:T(2,128)(2,1)} %reshape.233), calls=%async_computation.7 | async-start | bytes 3145728 | tf_op jit(solution)/shard_map/all_to_all | solution.py:90
  235.7 75.0 %all-to-all-start.4 = ((bf16[1,2,1,384,2048]{3,1,2,0,4:T(2,128)(2,1)}), bf16[1,2,1,384,2048]{3,1,2,0,4:T(2,128)(2,1)}, u32[]{:S(2)}, u32[]{:S(2)}) async-start(bf16[1,2,1,384,2048]{3,1,2,0,4:T(2,128)(2,1)} %copy.81), calls=%async_computation.6 | async-start | bytes 6291456 | tf_op jit(solution)/shard_map/all_to_all | solution.py:127
Sparse Core Ops, SparseCore 0:
  9.6 55.3 all-gather.2
  66.5 36.3 all-gather.4
  105.7 6.4 reduce-scatter.2
  137.3 7.8 reduce-scatter.4
